TPU v7x, 768 devices: a whole 4x8x12 slice. The times are simulated.
768 devices in a mesh: dp: 24 (over z, core), row: 16 (over x, y_lo), col: 2 (over y_hi).
Axes of the slice: x: 4, y: 8 (y_hi: 2, y_lo: 4; y = y_hi * 4 + y_lo), z: 12, core: 2. Of those that a mesh axis runs over, the one named last changes fastest.
Arguments:
- inputs: bfloat16 [98304, 4608], P(('dp', 'col'), 'row'), may hold values from -6 to 6
- grad_keys: bfloat16 [98304, 1024], P(('dp', 'row'), 'col'), may hold values from -6 to 6
- kv_weight: bfloat16 [4608, 1024], P('row', 'col'), may hold values from -0.09375 to 0.09375
Outputs:
- grad_inputs: bfloat16 [98304, 4608], P(('dp', 'col'), 'row')
- grad_weight: bfloat16 [4608, 1024], P(('row', 'dp'), 'col')
All inputs are finite; a program needn't handle non-finite values.
Results may differ from a plain program's by a relative error of at most 0.0051.
Values may be sent and summed in bfloat16 or wider, within the bound.
A program may use at most 32 MiB of HBM per device.

v0:
```python
import jax
import jax.numpy as jnp
from jax import lax
from jax.sharding import PartitionSpec as P


def contract_rows(left, right):
    return lax.dot_general(
        left, right, (((0,), (0,)), ((), ())), preferred_element_type=jnp.float32
    )


def contract_last(left, right):
    return lax.dot_general(
        left, right, (((1,), (1,)), ((), ())), preferred_element_type=jnp.float32
    )


def per_device(inputs, grad_keys, kv_weight):
    grads_all = lax.all_gather(grad_keys, "row", axis=0, tiled=True)
    rows_all = lax.all_gather(inputs, "col", axis=0, tiled=True)
    input_partial = contract_last(grads_all, kv_weight)
    grad_inputs = lax.psum_scatter(
        input_partial.astype(jnp.bfloat16), "col", scatter_dimension=0, tiled=True
    )
    replicas = lax.axis_size("dp")
    norm_factor = float(rows_all.shape[0] * replicas) ** (-0.5)
    weight_term = contract_rows(rows_all, grads_all)
    weight_sum = lax.psum_scatter(weight_term, "dp", scatter_dimension=0, tiled=True)
    grad_weight = (weight_sum * norm_factor).astype(jnp.bfloat16)
    return (grad_inputs, grad_weight)


def solution(mesh):
    in_specs = (P(("dp", "col"), "row"), P(("dp", "row"), "col"), P("row", "col"))
    out_specs = (P(("dp", "col"), "row"), P(("row", "dp"), "col"))
    return jax.shard_map(
        per_device, mesh=mesh, in_specs=in_specs, out_specs=out_specs, check_vma=False
    )
```

profile of v0, /device:TPU:1, one launch (start us, length us, event | category | flops | bytes accessed | tf_op | source)
XLA Modules:
  0.0 282.8 jit_solution(987228369028220368)
XLA Ops:
  7.2 0.0 copy-start
  7.2 0.0 all-gather.3.cloned.1.call-start
  7.2 0.7 all-gather.3.cloned.1.call-update
  7.9 0.0 all-gather.5.cloned.1.call-start
  8.0 0.7 all-gather.5.cloned.1.call-update
  8.7 0.0 reduce-scatter.4.cloned.1.call-start
  8.7 116.3 %all-gather.3.cloned.1.call-done = bf16[4096,512]{1,0:T(8,128)(2,1)} async-done(((bf16[256,512]{1,0:T(8,128)(2,1)}), bf16[4096,512]{1,0:T(8,128)(2,1)}) %all-gather.3.cloned.1.call-update) | async-done | bytes 4194320 | tf_op jit(solution)/shard_map/all_gather | solution.py:20
  125.0 5.1 %convolution_convert_fusion = bf16[4096,288]{0,1:T(8,128)(2,1)} fusion(bf16[4096,512]{1,0:T(8,128)(2,1)} %all-gather.3.cloned.1.call-done, bf16[288,512]{1,0:T(8,128)(2,1)S(1)} %copy-done), kind=kOutput, calls=%fused_computation | convolution fusion | flops 1209139200 | bytes 6848512 | tf_op jit(solution)/shard_map/dot_general | solution.py:14
  130.1 0.0 reduce-scatter.4.cloned.1.call-update
  130.2 71.2 %all-gather.5.cloned.1.call-done = bf16[4096,288]{0,1:T(8,128)(2,1)} async-done(((bf16[2048,288]{0,1:T(8,128)(2,1)}), bf16[4096,288]{0,1:T(8,128)(2,1)}) %all-gather.5.cloned.1.call-update) | async-done | bytes 2359312 | tf_op jit(solution)/shard_map/all_gather | solution.py:21
  201.3 4.3 %fusion.2 = f32[288,512]{1,0:T(8,128)S(1)} fusion(bf16[4096,288]{0,1:T(8,128)(2,1)} %all-gather.5.cloned.1.call-done, bf16[4096,512]{1,0:T(8,128)(2,1)} %all-gather.3.cloned.1.call-done), kind=kOutput, calls=%fused_computation.3 | convolution fusion | flops 1207959552 | bytes 7143424 | tf_op jit(solution)/shard_map/dot_general | solution.py:8
  205.6 41.6 %fusion = f32[16,512]{1,0:T(8,128)S(1)} fusion(f32[288,512]{1,0:T(8,128)S(1)} %fusion.2), kind=kCustom, calls=%all-reduce-scatter | all-reduce-scatter fusion | flops 196609 | bytes 626688
  247.2 4.0 %collective-permute-start.5 = (f32[12,512]{1,0:T(8,128)S(1)}, f32[12,512]{1,0:T(8,128)S(1)}, u32[]{:S(2)}, u32[]{:S(2)}) collective-permute-start(f32[12,512]{1,0:T(8,128)S(1)} %slice), channel_id=1, source_target_pairs={{0,192},{32,224},{64,256},{96,288},{128,320},{160,352},{192,384},{... | collective-permute-start | bytes 73736
  251.3 5.7 %collective-permute-start = (f32[16,512]{1,0:T(8,128)S(1)}, f32[16,512]{1,0:T(8,128)S(1)}, u32[]{:S(2)}, u32[]{:S(2)}) collective-permute-start(f32[16,512]{1,0:T(8,128)S(1)} %fusion), channel_id=1, source_target_pairs={{0,32},{32,64},{64,96},{96,128},{128,160},{160,192},{192,224},{224... | collective-permute-start | bytes 98312
  257.0 1.3 collective-permute-start.1
  258.3 2.3 collective-permute-start.2
  260.6 8.5 %collective-permute-start.3 = (f32[16,512]{1,0:T(8,128)S(1)}, f32[16,512]{1,0:T(8,128)S(1)}, u32[]{:S(2)}, u32[]{:S(2)}) collective-permute-start(f32[16,512]{1,0:T(8,128)S(1)} %fusion), channel_id=1, source_target_pairs={{0,128},{32,160},{64,192},{96,224},{128,256},{160,288},{192,320},{... | collective-permute-start | bytes 98312
  269.1 2.2 collective-permute-start.4
  271.3 1.3 dynamic-slice.4
  273.3 0.0 collective-permute-done
  273.3 0.0 collective-permute-done.1
  273.3 0.7 concatenate
  274.1 0.6 fusion.1
  274.7 1.6 reduce-scatter.4.cloned.1.call-done
  (6 shorter events, 0.0 us)
Async XLA Ops:
  7.2 117.9 %copy-start = (bf16[288,512]{1,0:T(8,128)(2,1)S(1)}, bf16[288,512]{1,0:T(8,128)(2,1)}, u32[]{:S(2)}) copy-start(bf16[288,512]{1,0:T(8,128)(2,1)} %param.5) | copy-start | bytes 884740
  7.2 117.9 %all-gather.3.cloned.1.call-start = ((), (), s32[]{:S(2)}) async-start(), calls=%async_computation.1 | async-start | bytes 4456448 | tf_op jit(solution)/shard_map/all_gather | solution.py:20
  7.9 193.4 %all-gather.5.cloned.1.call-start = ((), (), s32[]{:S(2)}) async-start(), calls=%async_computation.3 | async-start | bytes 3538944 | tf_op jit(solution)/shard_map/all_gather | solution.py:21
  8.7 267.6 %reduce-scatter.4.cloned.1.call-start = ((), (), s32[]{:S(2)}) async-start(), calls=%async_computation.2 | async-start | bytes 3538944 | tf_op jit(solution)/shard_map/reduce_scatter | solution.py:23
  247.2 21.9 %collective-permute-start.5 = (f32[12,512]{1,0:T(8,128)S(1)}, f32[12,512]{1,0:T(8,128)S(1)}, u32[]{:S(2)}, u32[]{:S(2)}) collective-permute-start(f32[12,512]{1,0:T(8,128)S(1)} %slice), channel_id=1, source_target_pairs={{0,192},{32,224},{64,256},{96,288},{128,320},{160,352},{192,384},{... | collective-permute-start | bytes 73736
  251.3 22.0 %collective-permute-start = (f32[16,512]{1,0:T(8,128)S(1)}, f32[16,512]{1,0:T(8,128)S(1)}, u32[]{:S(2)}, u32[]{:S(2)}) collective-permute-start(f32[16,512]{1,0:T(8,128)S(1)} %fusion), channel_id=1, source_target_pairs={{0,32},{32,64},{64,96},{96,128},{128,160},{160,192},{192,224},{224... | collective-permute-start | bytes 98312
  257.0 16.3 %collective-permute-start.1 = (f32[16,512]{1,0:T(8,128)S(1)}, f32[16,512]{1,0:T(8,128)S(1)}, u32[]{:S(2)}, u32[]{:S(2)}) collective-permute-start(f32[16,512]{1,0:T(8,128)S(1)} %fusion), channel_id=1, source_target_pairs={{0,64},{32,96},{64,128},{96,160},{128,192},{160,224},{192,256},{22... | collective-permute-start | bytes 98312
  258.3 15.0 %collective-permute-start.2 = (f32[16,512]{1,0:T(8,128)S(1)}, f32[16,512]{1,0:T(8,128)S(1)}, u32[]{:S(2)}, u32[]{:S(2)}) collective-permute-start(f32[16,512]{1,0:T(8,128)S(1)} %fusion), channel_id=1, source_target_pairs={{0,96},{32,128},{64,160},{96,192},{128,224},{160,256},{192,288},{2... | collective-permute-start | bytes 98312
  260.6 12.7 %collective-permute-start.3 = (f32[16,512]{1,0:T(8,128)S(1)}, f32[16,512]{1,0:T(8,128)S(1)}, u32[]{:S(2)}, u32[]{:S(2)}) collective-permute-start(f32[16,512]{1,0:T(8,128)S(1)} %fusion), channel_id=1, source_target_pairs={{0,128},{32,160},{64,192},{96,224},{128,256},{160,288},{192,320},{... | collective-permute-start | bytes 98312
  269.1 4.2 %collective-permute-start.4 = (f32[16,512]{1,0:T(8,128)S(1)}, f32[16,512]{1,0:T(8,128)S(1)}, u32[]{:S(2)}, u32[]{:S(2)}) collective-permute-start(f32[16,512]{1,0:T(8,128)S(1)} %fusion), channel_id=1, source_target_pairs={{0,160},{32,192},{64,224},{96,256},{128,288},{160,320},{192,352},{... | collective-permute-start | bytes 98312
Sparse Core Ops, SparseCore 0:
  10.4 114.6 all-gather.2
  127.4 73.8 all-gather.4
  205.0 71.2 reduce-scatter.3
where the time goes:
time: 283 us
  waiting for transfers between devices  190 us (67%)
  blocking collectives  41.6 us (15%)
  starting transfers between devices  24.2 us (9%)
  between operations  14.5 us (5%)
  matrix products  9.38 us (3%)
    all_gather x1, waiting for transfers between devices, per_device(): grads_all = lax.all_gather(grad_keys, 'row', axis=0, tiled=True)  116 us
    all_gather x1, waiting for transfers between devices, per_device(): rows_all = lax.all_gather(inputs, 'col', axis=0, tiled=True)  71.2 us
    unnamed x1, blocking collectives  41.6 us
    unnamed x6, starting transfers between devices  24.1 us
  transfers between devices with their start and end apart: 9, of which 3 were waited for; matrix products, arithmetic and copies ran while one was open for 19% of the time, Pallas kernels for 0%

commit v1 on v0

v1 whole, which is shorter than its diff:
```python
import functools

import jax
import jax.numpy as jnp
from jax import lax
from jax.experimental import pallas as pl
from jax.experimental.pallas import tpu as pltpu
from jax.sharding import PartitionSpec as P

MESH = pl.DeviceIdType.MESH
PASSES = 2
LINE = 4
Z = 12


def dot_rows(a, b):
    return lax.dot_general(a, b, (((1,), (0,)), ((), ())), preferred_element_type=jnp.float32)


def dot_last(a, b):
    return lax.dot_general(a, b, (((1,), (1,)), ((), ())), preferred_element_type=jnp.float32)


def kernel(
    norm, xt_hbm, gk_hbm, w_hbm, gi_hbm, gw_out,
    blocks, xs, w_own, w_far, acc, sib, z_send, z_recv, sums, near_in, far_in, gi_tiles,
    local_sem, send_sem, block_sem, w_sem, sib_sem, z_sem, fin_sem,
):
    rows, cols = gk_hbm.shape[0], gk_hbm.shape[1] // PASSES
    feats = w_hbm.shape[0]
    part = feats // Z
    dp, row, p = lax.axis_index("dp"), lax.axis_index("row"), lax.axis_index("col")
    z, core = dp // 2, dp % 2
    x, v = row // LINE, row % LINE
    u = (x + LINE - 2 * p) % LINE
    far = u // 2
    sibling = {"dp": 2 * z + 1 - core}
    partner = {"col": 1 - p}
    x_up = {"row": ((x + 1) % LINE) * LINE + v}
    x_down = {"row": ((x + LINE - 1) % LINE) * LINE + v}
    y_up, y_down = {"row": row + 1}, {"row": row - 1}

    started = []
    sends = iter(range(10_000))

    def send(src, dst, recv, device, when=None):
        copy = pltpu.make_async_remote_copy(
            src_ref=src, dst_ref=dst, send_sem=send_sem.at[next(sends)], recv_sem=recv,
            device_id=device, device_id_type=MESH,
        )
        started.append((copy, when))
        if when is None:
            copy.start()
        else:
            pl.when(when)(copy.start)

    def arrived(dst, recv, device, when=None):
        copy = pltpu.make_async_remote_copy(
            src_ref=dst, dst_ref=dst, send_sem=send_sem.at[0], recv_sem=recv,
            device_id=device, device_id_type=MESH,
        )
        if when is None:
            copy.wait_recv()
        else:
            pl.when(when)(copy.wait_recv)

    def order(line_far, k):
        upper = v // 2
        mirrored = v + upper * (3 - 2 * v)
        near_k = (mirrored, 1 - mirrored, 2, 3)[k]
        far_k = (3, 2, 0, 1)[k]
        low = line_far * far_k + (1 - line_far) * near_k
        return low + upper * (3 - 2 * low)

    def column_slot(uu, k):
        ff = uu // 2
        return ff * (20 - 4 * uu) + (1 - ff) * 4 * uu + order(ff, k)

    def half(s, slot, i):
        return blocks.at[s, slot, pl.ds(i * (rows // 2), rows // 2)]

    def accumulate(s, slot):
        h, t = slot // 8, slot % 8
        acc[s, h] += dot_rows(xs[t], blocks[s, slot])

    own_slot = 4 * u + v
    own = [
        pltpu.make_async_copy(gk_hbm.at[:, pl.ds(s * cols, cols)], blocks.at[s, own_slot], local_sem.at[s])
        for s in range(PASSES)
    ]
    tiles = xs.shape[0]
    loads = [
        pltpu.make_async_copy(xt_hbm.at[:, pl.ds(t * rows, rows)], xs.at[t], local_sem.at[PASSES + t])
        for t in range(tiles)
    ]
    load_w = pltpu.make_async_copy(w_hbm, w_own, local_sem.at[PASSES + tiles])
    is_near, is_far = far == 0, far == 1
    for copy in own:
        pl.when(is_near)(copy.start)

    far_u = u - 2
    far_x = (3 - far_u + 2 * (1 - p)) % LINE
    far_entry = 3 * (1 - v // 2)
    far_device = {"row": far_x * LINE + far_entry, "col": 1 - p}
    far_slot = 8 + 4 * far_u + v

    def start_far(s):
        send(
            gk_hbm.at[:, pl.ds(s * cols, cols)], blocks.at[s, far_slot], block_sem.at[s, far_slot, 0],
            far_device, is_far,
        )

    def column_step(s, k, first):
        j = order(far, k)
        slot = column_slot(u, k)
        here, sem = blocks.at[s, slot], block_sem.at[s, slot, 0]
        entry = far * 3 * (1 - j // 2) + (1 - far) * j
        if first:
            if k == 0:
                pl.when(is_near)(own[s].wait)
                arrived(here, sem, sibling, is_far)
            else:
                arrived(here, sem, sibling)
        send(here, here, sem, x_up)
        send(here, here, sem, x_down)
        send(here, here, sem, y_down, jnp.logical_and(v <= entry, v > 0))
        send(here, here, sem, y_up, jnp.logical_and(v >= entry, v < LINE - 1))

    def side_step(s, k):
        left = column_slot((u + LINE - 1) % LINE, k)
        right = column_slot((u + 1) % LINE, k)
        arrived(blocks.at[s, left], block_sem.at[s, left, 0], sibling)
        send(half(s, left, 0), half(s, left, 0), block_sem.at[s, left, 0], x_up)
        arrived(blocks.at[s, right], block_sem.at[s, right, 0], sibling)
        send(half(s, right, 1), half(s, right, 1), block_sem.at[s, right, 1], x_down)
        accumulate(s, left)
        accumulate(s, right)

    def opposite_step(s, k):
        slot = column_slot((u + 2) % LINE, k)
        for i in range(2):
            arrived(half(s, slot, i), block_sem.at[s, slot, i], sibling)
        accumulate(s, slot)

    def cores_start(s):
        send(acc.at[s, 1 - core], sib.at[s], sib_sem.at[s], sibling)

    def z_start(s):
        arrived(sib.at[s], sib_sem.at[s], sibling)
        acc[s, core] += sib[s]
        for zz in range(Z):
            z_send[s, zz] = acc[s, core, pl.ds(zz * part, part)].astype(jnp.bfloat16)
        for d in range(1, Z):
            to = (z + d) % Z
            send(z_send.at[s, to], z_recv.at[s, z], z_sem.at[s, z], {"dp": 2 * to + core})

    def z_finish(s):
        total = acc[s, core, pl.ds(pl.multiple_of(z * part, 8), part)]
        for d in range(1, Z):
            source = (z + Z - d) % Z
            arrived(z_recv.at[s, source], z_sem.at[s, source], sibling)
            total = total + z_recv[s, source].astype(jnp.float32)
        for i in range(2):
            sums[i, :, s * cols:(s + 1) * cols] = total[i * (part // 2):(i + 1) * (part // 2)]

    w_rows = feats // 2
    w_part = w_far.at[pl.ds(pl.multiple_of(core * w_rows, 16), w_rows)]
    w_other = w_far.at[pl.ds(pl.multiple_of((1 - core) * w_rows, 16), w_rows)]

    start_far(0)
    for copy in loads:
        copy.start()
    load_w.start()
    acc[...] = jnp.zeros_like(acc)
    for s in range(PASSES):
        for k in range(LINE):
            column_step(s, k, True)
            if s == 0 and k == 0:
                start_far(1)
                send(w_hbm.at[pl.ds(pl.multiple_of(core * w_rows, 16), w_rows)], w_part, w_sem.at[0], partner)
                for copy in loads:
                    copy.wait()
            side_step(s, k)
            accumulate(s, column_slot(u, k))
            if s == 1 and k == 0:
                z_start(0)
            if s == 0 and k == 3:
                arrived(w_part, w_sem.at[0], sibling)
                send(w_part, w_part, w_sem.at[1], sibling)
            if k > 0:
                opposite_step(s, k - 1)
        opposite_step(s, LINE - 1)
        cores_start(s)
    z_finish(0)
    load_w.wait()
    arrived(w_other, w_sem.at[1], sibling)
    z_start(1)

    def tile(t, carry):
        def term(weight, slot):
            total = dot_last(weight[:, :cols], blocks[0, slot])
            for s in range(1, PASSES):
                total = total + dot_last(weight[:, s * cols:(s + 1) * cols], blocks[s, slot])
            return total.astype(jnp.bfloat16).astype(jnp.float32)

        gi_tiles[t] = (term(w_own, t) + term(w_far, t + 8)).astype(jnp.bfloat16)
        return carry

    lax.fori_loop(0, tiles, tile, 0)
    stores = [
        pltpu.make_async_copy(gi_tiles.at[t], gi_hbm.at[:, pl.ds(t * rows, rows)], local_sem.at[t])
        for t in range(tiles)
    ]
    for copy in stores:
        copy.start()

    z_finish(1)
    is_zero, is_one = core == 0, core == 1
    send(sums.at[1], near_in, fin_sem.at[0], sibling, is_zero)
    send(sums.at[0], far_in, fin_sem.at[1], {"dp": 2 * z, "col": 1 - p}, is_one)
    send(sums.at[1], far_in, fin_sem.at[1], {"dp": 2 * z + 1, "col": 1 - p}, is_one)

    arrived(far_in, fin_sem.at[1], sibling)

    @pl.when(is_zero)
    def _():
        gw_out[...] = ((sums[0] + far_in[...]) * norm).astype(jnp.bfloat16)

    @pl.when(is_one)
    def _():
        arrived(near_in, fin_sem.at[0], sibling)
        gw_out[...] = ((near_in[...] + far_in[...]) * norm).astype(jnp.bfloat16)

    for copy in stores:
        copy.wait()
    for copy, when in started:
        if when is None:
            copy.wait_send()
        else:
            pl.when(when)(copy.wait_send)


def per_device(inputs, grad_keys, kv_weight):
    tokens, feats = inputs.shape
    rows, width = grad_keys.shape
    cols = width // PASSES
    tiles = tokens // rows
    replicas = lax.axis_size("dp")
    part = feats // Z
    norm = float(tokens * lax.axis_size("col") * replicas) ** (-0.5)
    bf16, f32 = jnp.bfloat16, jnp.float32
    hbm = pl.BlockSpec(memory_space=pl.ANY)
    gi, gw = pl.pallas_call(
        functools.partial(kernel, norm),
        out_shape=(
            jax.ShapeDtypeStruct((feats, tokens), bf16),
            jax.ShapeDtypeStruct((feats // replicas, width), bf16),
        ),
        in_specs=[hbm] * 3,
        out_specs=(hbm, pl.BlockSpec(memory_space=pltpu.VMEM)),
        scratch_shapes=[
            pltpu.VMEM((PASSES, 16, rows, cols), bf16),
            pltpu.VMEM((tiles, feats, rows), bf16),
            pltpu.VMEM((feats, width), bf16),
            pltpu.VMEM((feats, width), bf16),
            pltpu.VMEM((PASSES, 2, feats, cols), f32),
            pltpu.VMEM((PASSES, feats, cols), f32),
            pltpu.VMEM((PASSES, Z, part, cols), bf16),
            pltpu.VMEM((PASSES, Z, part, cols), bf16),
            pltpu.VMEM((2, part // 2, width), f32),
            pltpu.VMEM((part // 2, width), f32),
            pltpu.VMEM((part // 2, width), f32),
            pltpu.VMEM((tiles, feats, rows), bf16),
            pltpu.SemaphoreType.DMA((PASSES + tiles + 1,)),
            pltpu.SemaphoreType.DMA((96,)),
            pltpu.SemaphoreType.DMA((PASSES, 16, 2)),
            pltpu.SemaphoreType.DMA((2,)),
            pltpu.SemaphoreType.DMA((PASSES,)),
            pltpu.SemaphoreType.DMA((PASSES, Z)),
            pltpu.SemaphoreType.DMA((2,)),
        ],
        compiler_params=pltpu.CompilerParams(has_side_effects=True),
    )(inputs.T, grad_keys, kv_weight)
    return gi.T, gw


def solution(mesh):
    in_specs = (P(("dp", "col"), "row"), P(("dp", "row"), "col"), P("row", "col"))
    out_specs = (P(("dp", "col"), "row"), P(("row", "dp"), "col"))
    return jax.shard_map(
        per_device, mesh=mesh, in_specs=in_specs, out_specs=out_specs, check_vma=False
    )
```

time: 283 us -> 136 us (0.48)
  waiting for transfers between devices: 190 us -> 0 us
  Pallas kernels: 0 us -> 133 us
  blocking collectives: 41.6 us -> 0 us
  starting transfers between devices: 24.2 us -> 0 us
  between operations: 14.5 us -> 0.65 us
  matrix products: 9.38 us -> 0 us
    all_gather x2 -> x0, waiting for transfers between devices: 187 us -> none  [the longest x1 116 us: per_device(): grads_all = lax.all_gather(grad_keys, 'row', axis=0, tiled=True)]
    pallas_call x0 -> x1, Pallas kernels: none -> 133 us  [per_device(): pl.pallas_call(functools.partial(kernel, norm), out_shape=(jax.ShapeDtype...]
    unnamed x1 -> x0, blocking collectives: 41.6 us -> none
    unnamed x6 -> x0, starting transfers between devices: 24.1 us -> none
    dot_general x2 -> x0, matrix products: 9.38 us -> none  [the longest x1 5.1 us: contract_last(): lax.dot_general(left, right, (((1,), (1,)), ((), ())), preferred_element_...]
  transfers between devices with their start and end apart: 9 -> 0, of which waited for: 3 -> 0; matrix products, arithmetic and copies ran while one was open for 19% -> 0% of each run, Pallas kernels for 0% -> 0%
where the time goes in v1:
time: 136 us
  Pallas kernels  133 us (98%)
  local copies, waits for them, and re-layouts  3.02 us (2%)
    pallas_call x1, Pallas kernels, per_device(): pl.pallas_call(functools.partial(kernel, norm), out_shape=(jax.ShapeDtype...  133 us
    unnamed x4, local copies, waits for them, and re-layouts  3.02 us

profile of v1, /device:TPU:1, one launch (start us, length us, event | category | flops | bytes accessed | tf_op | source)
XLA Modules:
  0.0 136.2 jit_solution(4296116664309905608)
XLA Ops:
  0.6 132.5 %shard_map.50 = (bf16[288,2048]{1,0:T(8,128)(2,1)}, bf16[12,512]{1,0:T(8,128)(2,1)}) custom-call(bf16[288,2048]{1,0:T(8,128)(2,1)} %bitcast.3, bf16[256,512]{1,0:T(8,128)(2,1)} %gk_hbm.1, bf16[288,512]{1,0:T(8,128)(2,1)} %w_hbm.1), custom_call_target="tpu_custom_call" | custom-call | tf_op jit(solution)/shard_map/pallas_call | solution.py:253
  133.2 0.0 copy-start
  133.2 2.4 %copy.7 = bf16[2048,288]{0,1:T(8,128)(2,1)} copy(bf16[2048,288]{0,1:T(8,128)(2,1)} %bitcast.2) | data formatting | bytes 2359296
  135.6 0.0 copy-done
  135.6 0.6 copy.8
Async XLA Ops:
  133.2 2.4 %copy-start = (bf16[12,512]{1,0:T(8,128)(2,1)S(1)}, bf16[12,512]{1,0:T(8,128)(2,1)}, u32[]{:S(2)}) copy-start(bf16[12,512]{1,0:T(8,128)(2,1)} %get-tuple-element.9) | copy-start | bytes 36868

commit v2 on v1

--- a/solution.py
+++ b/solution.py
@@ -7,6 +7,30 @@
 from jax.experimental.pallas import tpu as pltpu
 from jax.sharding import PartitionSpec as P
 
+
+def gather_program():
+    program = [("F", s) for s in range(2)]
+    for i in range(12):
+        if i < 8:
+            program.append(("Y", i))
+        if i == 0:
+            program.append(("W", 0))
+        if i < 8:
+            program.append(("X", i))
+        if 2 <= i < 10:
+            program += [("L", i - 2), ("R", i - 2)]
+        if i == 4:
+            program.append(("V", 0))
+        if i >= 4:
+            program.append(("O", i - 4))
+        if i == 7:
+            program.append(("C", 0))
+        if i == 9:
+            program.append(("Z", 0))
+    return program + [("C", 1), ("E", 0)]
+
+
+PROGRAM = gather_program()
 MESH = pl.DeviceIdType.MESH
 PASSES = 2
 LINE = 4
@@ -110,31 +134,37 @@
             far_device, is_far,
         )
 
-    def column_step(s, k, first):
+    def line_step(s, k):
         j = order(far, k)
         slot = column_slot(u, k)
         here, sem = blocks.at[s, slot], block_sem.at[s, slot, 0]
         entry = far * 3 * (1 - j // 2) + (1 - far) * j
-        if first:
-            if k == 0:
-                pl.when(is_near)(own[s].wait)
-                arrived(here, sem, sibling, is_far)
-            else:
-                arrived(here, sem, sibling)
+        if k == 0:
+            pl.when(is_near)(own[s].wait)
+            arrived(here, sem, sibling, is_far)
+        else:
+            arrived(here, sem, sibling)
+        send(here, here, sem, y_down, jnp.logical_and(v <= entry, v > 0))
+        send(here, here, sem, y_up, jnp.logical_and(v >= entry, v < LINE - 1))
+
+    def ring_step(s, k):
+        slot = column_slot(u, k)
+        here, sem = blocks.at[s, slot], block_sem.at[s, slot, 0]
         send(here, here, sem, x_up)
         send(here, here, sem, x_down)
-        send(here, here, sem, y_down, jnp.logical_and(v <= entry, v > 0))
-        send(here, here, sem, y_up, jnp.logical_and(v >= entry, v < LINE - 1))
-
-    def side_step(s, k):
-        left = column_slot((u + LINE - 1) % LINE, k)
-        right = column_slot((u + 1) % LINE, k)
-        arrived(blocks.at[s, left], block_sem.at[s, left, 0], sibling)
-        send(half(s, left, 0), half(s, left, 0), block_sem.at[s, left, 0], x_up)
-        arrived(blocks.at[s, right], block_sem.at[s, right, 0], sibling)
-        send(half(s, right, 1), half(s, right, 1), block_sem.at[s, right, 1], x_down)
-        accumulate(s, left)
-        accumulate(s, right)
+        accumulate(s, slot)
+
+    def left_step(s, k):
+        slot = column_slot((u + LINE - 1) % LINE, k)
+        arrived(blocks.at[s, slot], block_sem.at[s, slot, 0], sibling)
+        send(half(s, slot, 0), half(s, slot, 0), block_sem.at[s, slot, 0], x_up)
+        accumulate(s, slot)
+
+    def right_step(s, k):
+        slot = column_slot((u + 1) % LINE, k)
+        arrived(blocks.at[s, slot], block_sem.at[s, slot, 0], sibling)
+        send(half(s, slot, 1), half(s, slot, 1), block_sem.at[s, slot, 1], x_down)
+        accumulate(s, slot)
 
     def opposite_step(s, k):
         slot = column_slot((u + 2) % LINE, k)
@@ -167,31 +197,55 @@
     w_part = w_far.at[pl.ds(pl.multiple_of(core * w_rows, 16), w_rows)]
     w_other = w_far.at[pl.ds(pl.multiple_of((1 - core) * w_rows, 16), w_rows)]
 
-    start_far(0)
+    barrier = pltpu.get_barrier_semaphore()
+
+    def greet(device, when=None):
+        def signal():
+            pl.semaphore_signal(barrier, inc=1, device_id=device, device_id_type=MESH)
+
+        if when is None:
+            signal()
+        else:
+            pl.when(when)(signal)
+
+    greet(x_up)
+    greet(x_down)
+    greet(sibling)
+    for k in range(2):
+        greet({"dp": 2 * z + k, "col": 1 - p})
+    for step in (1, 7):
+        y = (4 * p + v + step) % 8
+        greet({"row": x * LINE + y % LINE, "col": y // LINE})
+    for d in range(1, Z):
+        greet({"dp": 2 * ((z + d) % Z) + core})
+    far_greets = jnp.logical_and(is_far, v % 3 == 0)
+    for i in range(2):
+        source_x = (5 - u + 2 * (1 - p)) % LINE
+        greet({"row": source_x * LINE + 2 * (1 - v // 3) + i, "col": 1 - p}, far_greets)
+
     for copy in loads:
         copy.start()
     load_w.start()
     acc[...] = jnp.zeros_like(acc)
-    for s in range(PASSES):
-        for k in range(LINE):
-            column_step(s, k, True)
-            if s == 0 and k == 0:
-                start_far(1)
-                send(w_hbm.at[pl.ds(pl.multiple_of(core * w_rows, 16), w_rows)], w_part, w_sem.at[0], partner)
-                for copy in loads:
-                    copy.wait()
-            side_step(s, k)
-            accumulate(s, column_slot(u, k))
-            if s == 1 and k == 0:
-                z_start(0)
-            if s == 0 and k == 3:
-                arrived(w_part, w_sem.at[0], sibling)
-                send(w_part, w_part, w_sem.at[1], sibling)
-            if k > 0:
-                opposite_step(s, k - 1)
-        opposite_step(s, LINE - 1)
-        cores_start(s)
-    z_finish(0)
+    pl.semaphore_wait(barrier, 18 + far)
+    def weight_send():
+        send(w_hbm.at[pl.ds(pl.multiple_of(core * w_rows, 16), w_rows)], w_part, w_sem.at[0], partner)
+        for copy in loads:
+            copy.wait()
+
+    def weight_forward():
+        arrived(w_part, w_sem.at[0], sibling)
+        send(w_part, w_part, w_sem.at[1], sibling)
+
+    steps = dict(
+        F=lambda i: start_far(i), W=lambda i: weight_send(), V=lambda i: weight_forward(),
+        Y=lambda i: line_step(*divmod(i, LINE)), X=lambda i: ring_step(*divmod(i, LINE)),
+        L=lambda i: left_step(*divmod(i, LINE)), R=lambda i: right_step(*divmod(i, LINE)),
+        O=lambda i: opposite_step(*divmod(i, LINE)),
+        C=cores_start, Z=z_start, E=z_finish,
+    )
+    for name, i in PROGRAM:
+        steps[name](i)
     load_w.wait()
     arrived(w_other, w_sem.at[1], sibling)
     z_start(1)
@@ -279,7 +333,7 @@
             pltpu.SemaphoreType.DMA((PASSES, Z)),
             pltpu.SemaphoreType.DMA((2,)),
         ],
-        compiler_params=pltpu.CompilerParams(has_side_effects=True),
+        compiler_params=pltpu.CompilerParams(collective_id=0, has_side_effects=True),
     )(inputs.T, grad_keys, kv_weight)
     return gi.T, gw
 

time: 136 us -> 97.5 us (0.72)
  Pallas kernels: 133 us -> 93.7 us
    pallas_call x1, Pallas kernels: 133 us -> 93.7 us  [per_device(): pl.pallas_call(functools.partial(kernel, norm), out_shape=(jax.ShapeDtype...]
where the time goes in v2:
time: 97.5 us; the launch traced here: 97.4 us
  Pallas kernels  93.7 us (96%)
  local copies, waits for them, and re-layouts  3.02 us (3%)
    pallas_call x1, Pallas kernels, per_device(): pl.pallas_call(functools.partial(kernel, norm), out_shape=(jax.ShapeDtype...  93.7 us
    unnamed x4, local copies, waits for them, and re-layouts  3.02 us

profile of v2, /device:TPU:1, one launch (start us, length us, event | category | flops | bytes accessed | tf_op | source)
XLA Modules:
  0.0 97.4 jit_solution(3532129861163034607)
XLA Ops:
  0.6 93.7 %shard_map.50 = (bf16[288,2048]{1,0:T(8,128)(2,1)}, bf16[12,512]{1,0:T(8,128)(2,1)}) custom-call(bf16[288,2048]{1,0:T(8,128)(2,1)} %bitcast.3, bf16[256,512]{1,0:T(8,128)(2,1)} %gk_hbm.1, bf16[288,512]{1,0:T(8,128)(2,1)} %w_hbm.1), custom_call_target="tpu_custom_call" | custom-call | tf_op jit(solution)/shard_map/pallas_call | solution.py:307
  94.3 0.0 copy-start
  94.3 2.4 %copy.7 = bf16[2048,288]{0,1:T(8,128)(2,1)} copy(bf16[2048,288]{0,1:T(8,128)(2,1)} %bitcast.2) | data formatting | bytes 2359296
  96.8 0.0 copy-done
  96.8 0.6 copy.8
Async XLA Ops:
  94.3 2.4 %copy-start = (bf16[12,512]{1,0:T(8,128)(2,1)S(1)}, bf16[12,512]{1,0:T(8,128)(2,1)}, u32[]{:S(2)}) copy-start(bf16[12,512]{1,0:T(8,128)(2,1)} %get-tuple-element.9) | copy-start | bytes 36868

commit v3 on v2

--- a/solution.py
+++ b/solution.py
@@ -19,6 +19,8 @@
             program.append(("X", i))
         if 2 <= i < 10:
             program += [("L", i - 2), ("R", i - 2)]
+        if 1 <= i <= 6:
+            program.append(("T", i))
         if i == 4:
             program.append(("V", 0))
         if i >= 4:
@@ -48,7 +50,7 @@
 def kernel(
     norm, xt_hbm, gk_hbm, w_hbm, gi_hbm, gw_out,
     blocks, xs, w_own, w_far, acc, sib, z_send, z_recv, sums, near_in, far_in, gi_tiles,
-    local_sem, send_sem, block_sem, w_sem, sib_sem, z_sem, fin_sem,
+    local_sem, send_sem, block_sem, w_sem, sib_sem, z_sem, fin_sem, token_sem,
 ):
     rows, cols = gk_hbm.shape[0], gk_hbm.shape[1] // PASSES
     feats = w_hbm.shape[0]
@@ -216,8 +218,9 @@
     for step in (1, 7):
         y = (4 * p + v + step) % 8
         greet({"row": x * LINE + y % LINE, "col": y // LINE})
-    for d in range(1, Z):
-        greet({"dp": 2 * ((z + d) % Z) + core})
+    z_up, z_down = {"dp": 2 * ((z + 1) % Z) + core}, {"dp": 2 * ((z + Z - 1) % Z) + core}
+    greet(z_up)
+    greet(z_down)
     far_greets = jnp.logical_and(is_far, v % 3 == 0)
     for i in range(2):
         source_x = (5 - u + 2 * (1 - p)) % LINE
@@ -227,7 +230,7 @@
         copy.start()
     load_w.start()
     acc[...] = jnp.zeros_like(acc)
-    pl.semaphore_wait(barrier, 18 + far)
+    pl.semaphore_wait(barrier, 9 + far)
     def weight_send():
         send(w_hbm.at[pl.ds(pl.multiple_of(core * w_rows, 16), w_rows)], w_part, w_sem.at[0], partner)
         for copy in loads:
@@ -237,7 +240,15 @@
         arrived(w_part, w_sem.at[0], sibling)
         send(w_part, w_part, w_sem.at[1], sibling)
 
+    def token_round(r):
+        for i, (device, rounds) in enumerate(((z_up, 5), (z_down, 4))):
+            if 1 <= r - 1 <= rounds:
+                pl.semaphore_wait(token_sem.at[i, r - 1], 1)
+            if r <= rounds:
+                pl.semaphore_signal(token_sem.at[i, r], inc=1, device_id=device, device_id_type=MESH)
+
     steps = dict(
+        T=token_round,
         F=lambda i: start_far(i), W=lambda i: weight_send(), V=lambda i: weight_forward(),
         Y=lambda i: line_step(*divmod(i, LINE)), X=lambda i: ring_step(*divmod(i, LINE)),
         L=lambda i: left_step(*divmod(i, LINE)), R=lambda i: right_step(*divmod(i, LINE)),
@@ -332,6 +343,7 @@
             pltpu.SemaphoreType.DMA((PASSES,)),
             pltpu.SemaphoreType.DMA((PASSES, Z)),
             pltpu.SemaphoreType.DMA((2,)),
+            pltpu.SemaphoreType.REGULAR((2, 6)),
         ],
         compiler_params=pltpu.CompilerParams(collective_id=0, has_side_effects=True),
     )(inputs.T, grad_keys, kv_weight)

time: 97.5 us -> 94.5 us (0.969)
  Pallas kernels: 93.7 us -> 90.6 us
    pallas_call x1, Pallas kernels: 93.7 us -> 90.6 us  [per_device(): pl.pallas_call(functools.partial(kernel, norm), out_shape=(jax.ShapeDtype...]
where the time goes in v3:
time: 94.5 us; the launch traced here: 94.3 us
  Pallas kernels  90.6 us (96%)
  local copies, waits for them, and re-layouts  3.02 us (3%)
    pallas_call x1, Pallas kernels, per_device(): pl.pallas_call(functools.partial(kernel, norm), out_shape=(jax.ShapeDtype...  90.6 us
    unnamed x4, local copies, waits for them, and re-layouts  3.02 us

profile of v3, /device:TPU:1, one launch (start us, length us, event | category | flops | bytes accessed | tf_op | source)
XLA Modules:
  0.0 94.3 jit_solution(7681659151075296523)
XLA Ops:
  0.6 90.6 %shard_map.50 = (bf16[288,2048]{1,0:T(8,128)(2,1)}, bf16[12,512]{1,0:T(8,128)(2,1)}) custom-call(bf16[288,2048]{1,0:T(8,128)(2,1)} %bitcast.3, bf16[256,512]{1,0:T(8,128)(2,1)} %gk_hbm.1, bf16[288,512]{1,0:T(8,128)(2,1)} %w_hbm.1), custom_call_target="tpu_custom_call" | custom-call | tf_op jit(solution)/shard_map/pallas_call | solution.py:318
  91.3 0.0 copy-start
  91.3 2.4 %copy.7 = bf16[2048,288]{0,1:T(8,128)(2,1)} copy(bf16[2048,288]{0,1:T(8,128)(2,1)} %bitcast.2) | data formatting | bytes 2359296
  93.7 0.0 copy-done
  93.7 0.6 copy.8
Async XLA Ops:
  91.3 2.4 %copy-start = (bf16[12,512]{1,0:T(8,128)(2,1)S(1)}, bf16[12,512]{1,0:T(8,128)(2,1)}, u32[]{:S(2)}) copy-start(bf16[12,512]{1,0:T(8,128)(2,1)} %get-tuple-element.9) | copy-start | bytes 36868

commit v4 on v3

--- a/solution.py
+++ b/solution.py
@@ -7,32 +7,13 @@
 from jax.experimental.pallas import tpu as pltpu
 from jax.sharding import PartitionSpec as P
 
-
-def gather_program():
-    program = [("F", s) for s in range(2)]
-    for i in range(12):
-        if i < 8:
-            program.append(("Y", i))
-        if i == 0:
-            program.append(("W", 0))
-        if i < 8:
-            program.append(("X", i))
-        if 2 <= i < 10:
-            program += [("L", i - 2), ("R", i - 2)]
-        if 1 <= i <= 6:
-            program.append(("T", i))
-        if i == 4:
-            program.append(("V", 0))
-        if i >= 4:
-            program.append(("O", i - 4))
-        if i == 7:
-            program.append(("C", 0))
-        if i == 9:
-            program.append(("Z", 0))
-    return program + [("C", 1), ("E", 0)]
-
-
-PROGRAM = gather_program()
+PROGRAM = [
+    ("F", 0), ("F", 1), ("Y", 0), ("D", 0), ("X", 0), ("Y", 1), ("X", 1), ("R", 0), ("Y", 4), ("L", 0), ("X", 4),
+    ("T", 1), ("L", 1), ("R", 1), ("Y", 5), ("T", 2), ("X", 5), ("Y", 2), ("X", 2), ("T", 3), ("Y", 3), ("X", 3),
+    ("Y", 6), ("T", 4), ("X", 6), ("Y", 7), ("W", 0), ("L", 3), ("T", 5), ("R", 3), ("R", 2), ("L", 2), ("T", 6),
+    ("X", 7), ("O", 1), ("R", 4), ("L", 5), ("L", 6), ("O", 0), ("O", 3), ("O", 2), ("C", 0), ("R", 6), ("L", 4),
+    ("R", 5), ("R", 7), ("V", 0), ("L", 7), ("Z", 0), ("O", 4), ("O", 5), ("O", 6), ("O", 7), ("C", 1), ("E", 0),
+]
 MESH = pl.DeviceIdType.MESH
 PASSES = 2
 LINE = 4
@@ -231,10 +212,12 @@
     load_w.start()
     acc[...] = jnp.zeros_like(acc)
     pl.semaphore_wait(barrier, 9 + far)
+    def wait_loads():
+        for copy in loads:
+            copy.wait()
+
     def weight_send():
         send(w_hbm.at[pl.ds(pl.multiple_of(core * w_rows, 16), w_rows)], w_part, w_sem.at[0], partner)
-        for copy in loads:
-            copy.wait()
 
     def weight_forward():
         arrived(w_part, w_sem.at[0], sibling)
@@ -248,7 +231,7 @@
                 pl.semaphore_signal(token_sem.at[i, r], inc=1, device_id=device, device_id_type=MESH)
 
     steps = dict(
-        T=token_round,
+        T=token_round, D=lambda i: wait_loads(),
         F=lambda i: start_far(i), W=lambda i: weight_send(), V=lambda i: weight_forward(),
         Y=lambda i: line_step(*divmod(i, LINE)), X=lambda i: ring_step(*divmod(i, LINE)),
         L=lambda i: left_step(*divmod(i, LINE)), R=lambda i: right_step(*divmod(i, LINE)),

time: 94.5 us -> 92.1 us (0.975)
  Pallas kernels: 90.6 us -> 87.9 us
    pallas_call x1, Pallas kernels: 90.6 us -> 87.9 us  [per_device(): pl.pallas_call(functools.partial(kernel, norm), out_shape=(jax.ShapeDtype...]
where the time goes in v4:
time: 92.1 us; the launch traced here: 91.6 us
  Pallas kernels  87.9 us (95%)
  local copies, waits for them, and re-layouts  3.02 us (3%)
    pallas_call x1, Pallas kernels, per_device(): pl.pallas_call(functools.partial(kernel, norm), out_shape=(jax.ShapeDtype...  87.9 us
    unnamed x4, local copies, waits for them, and re-layouts  3.02 us

profile of v4, /device:TPU:1, one launch (start us, length us, event | category | flops | bytes accessed | tf_op | source)
XLA Modules:
  0.0 91.6 jit_solution(1564493868343939323)
XLA Ops:
  0.6 87.9 %shard_map.50 = (bf16[288,2048]{1,0:T(8,128)(2,1)}, bf16[12,512]{1,0:T(8,128)(2,1)}) custom-call(bf16[288,2048]{1,0:T(8,128)(2,1)} %bitcast.3, bf16[256,512]{1,0:T(8,128)(2,1)} %gk_hbm.1, bf16[288,512]{1,0:T(8,128)(2,1)} %w_hbm.1), custom_call_target="tpu_custom_call" | custom-call | tf_op jit(solution)/shard_map/pallas_call | solution.py:301
  88.5 0.0 copy-start
  88.6 2.4 %copy.7 = bf16[2048,288]{0,1:T(8,128)(2,1)} copy(bf16[2048,288]{0,1:T(8,128)(2,1)} %bitcast.2) | data formatting | bytes 2359296
  91.0 0.0 copy-done
  91.0 0.6 copy.8
Async XLA Ops:
  88.5 2.4 %copy-start = (bf16[12,512]{1,0:T(8,128)(2,1)S(1)}, bf16[12,512]{1,0:T(8,128)(2,1)}, u32[]{:S(2)}) copy-start(bf16[12,512]{1,0:T(8,128)(2,1)} %get-tuple-element.9) | copy-start | bytes 36868
